TPU v7x, 32 devices: a whole 2x2x4 slice. The times are simulated.
32 devices in a mesh: dp: 8 (over y, x, core), tensor: 4 (over z).
Axes of the slice: x: 2, y: 2, z: 4, core: 2. Of those that a mesh axis runs over, the one named last changes fastest.
Arguments:
- enc_hidden: bfloat16 [16384, 4096], P(('dp', 'tensor')), parts along dimension 0, may hold values from -6 to 6
- enc_gain: float32 [4096], replicated, may hold values from 0.1 to 1.9
- dec_hidden: bfloat16 [4096, 4096], P(('dp', 'tensor')), parts along dimension 0, may hold values from -6 to 6
- dec_gain: float32 [4096], replicated, may hold values from 0.8 to 12, as said below
- w_query: bfloat16 [4096, 4096], P(None, 'tensor'), may hold values from -0.046875 to 0.046875
- w_key: bfloat16 [4096, 4096], P(None, 'tensor'), may hold values from -0.09375 to 0.09375
- w_value: bfloat16 [4096, 4096], P(None, 'tensor'), may hold values from -0.09375 to 0.09375
- w_out: bfloat16 [4096, 4096], P('tensor'), may hold values from -0.75 to 0.75
- enc_length: int32 [8], P('dp'), parts along dimension 0, may hold values from 1024 to 2048
- dec_length: int32 [8], P('dp'), parts along dimension 0, may hold values from 256 to 512
Outputs:
- memory: bfloat16 [16384, 4096], P(('dp', 'tensor')), parts along dimension 0
- cross_out: bfloat16 [4096, 4096], P(('dp', 'tensor')), parts along dimension 0
There are 8 independent parts, one for each index of `dp`. A program takes and returns all parts, laid end to end along the dimension named above; an argument that names none is the same for every part. Nothing has to cross between parts.
Inputs may be any that keep to these rules, and one draw needn't show every extreme that they name: `dec_gain`: positive.
All inputs are finite; a program needn't handle non-finite values.
Results may differ from a plain program's by a relative error of at most 0.02.
The roundings to bfloat16 on the way count: a program that leaves them out, or rounds other values in their place, can miss the bound.
Values may be sent and summed in bfloat16 or wider, within the bound.
No kernel may reach another device: no remote copies, remote signals or barrier semaphores. Data moves between devices by JAX's collectives and lax.ppermute only.
A program may use at most 192 MiB of HBM per device.

v0:
```python
import jax
import jax.numpy as jnp
from jax import lax
from jax.sharding import PartitionSpec as P

HEAD_DIM = 64
ENC_LEN = 2048
DEC_LEN = 512


def rms_norm(values, gain):
    wide = values.astype(jnp.float32)
    mean_sq = jnp.mean(wide * wide, axis=-1, keepdims=True)
    return (wide * lax.rsqrt(mean_sq + 1e-06) * gain).astype(jnp.bfloat16)


def shards(
    enc_hidden,
    enc_gain,
    dec_hidden,
    dec_gain,
    w_query,
    w_key,
    w_value,
    w_out,
    enc_length,
    dec_length,
):
    memory = rms_norm(enc_hidden, enc_gain)
    normed = rms_norm(dec_hidden, dec_gain)
    local_width = w_query.shape[1]
    local_heads = local_width // HEAD_DIM
    dec_rows = dec_hidden.shape[0]
    all_normed = lax.all_gather(normed, "tensor", axis=0, tiled=True)
    queries = jnp.dot(all_normed, w_query, preferred_element_type=jnp.float32).astype(jnp.bfloat16)
    q_heads = queries.reshape(DEC_LEN, local_heads, HEAD_DIM)
    segment = lax.all_gather(memory, "tensor", axis=0, tiled=True)
    key_part = jnp.dot(segment, w_key, preferred_element_type=jnp.float32).astype(jnp.bfloat16)
    value_part = jnp.dot(segment, w_value, preferred_element_type=jnp.float32).astype(jnp.bfloat16)
    paired = jnp.concatenate([key_part, value_part], axis=1)
    key_rows = paired[:, :local_width]
    value_rows = paired[:, local_width:]
    k_heads = key_rows.reshape(ENC_LEN, local_heads, HEAD_DIM)
    scores = jnp.einsum("qhd,khd->hqk", q_heads, k_heads, preferred_element_type=jnp.float32)
    valid_keys = jnp.arange(ENC_LEN, dtype=jnp.int32) < enc_length[0]
    scores = jnp.where(valid_keys[None, None, :], scores, -jnp.inf)
    weights = jax.nn.softmax(scores, axis=-1).astype(jnp.bfloat16)
    v_heads = value_rows.reshape(ENC_LEN, local_heads, HEAD_DIM)
    context = jnp.einsum("hqk,khd->qhd", weights, v_heads, preferred_element_type=jnp.float32)
    context = context.astype(jnp.bfloat16).reshape(DEC_LEN, local_width)
    projected = lax.psum_scatter(
        jnp.dot(context, w_out, preferred_element_type=jnp.float32).astype(jnp.bfloat16),
        "tensor",
        scatter_dimension=0,
        tiled=True,
    ).astype(jnp.float32)
    row_ids = lax.axis_index("tensor") * dec_rows + jnp.arange(dec_rows, dtype=jnp.int32)
    live_rows = row_ids < dec_length[0]
    cross_out = jnp.where(live_rows[:, None], projected, 0.0).astype(jnp.bfloat16)
    return (memory, cross_out)


def solution(mesh):
    placed = (
        P(("dp", "tensor"), None),
        P(),
        P(("dp", "tensor"), None),
        P(),
        P(None, "tensor"),
        P(None, "tensor"),
        P(None, "tensor"),
        P("tensor", None),
        P("dp"),
        P("dp"),
    )
    return jax.shard_map(
        shards,
        mesh=mesh,
        in_specs=placed,
        out_specs=(P(("dp", "tensor"), None), P(("dp", "tensor"), None)),
        check_vma=False,
    )
```

profile of v0, /device:TPU:0, one launch (start us, length us, event | category | flops | bytes accessed | tf_op | source)
XLA Modules:
  0.0 576.0 jit_solution(13626997619669954659)
XLA Ops:
  7.2 0.0 copy-start
  7.2 0.0 all-gather.5.cloned.1.call-start
  7.2 1.5 fusion.10
  8.7 2.5 fusion.12
  11.3 0.0 all-gather.5.cloned.1.call-update
  11.3 0.0 all-gather.3.cloned.1.call-start
  11.4 3.1 fusion.7
  14.4 0.0 copy-done
  14.5 5.8 %fusion.9 = bf16[512,4096]{1,0:T(8,128)(2,1)} fusion(bf16[512,4096]{1,0:T(8,128)(2,1)} %param.10, f32[4096]{0:T(1024)S(1)} %copy-done, f32[512]{0:T(512)S(1)} %add_rsqrt_fusion), kind=kLoop, calls=%fused_computation.12 | loop fusion | flops 8388608 | bytes 8407040 | tf_op jit(solution)/shard_map/convert_element_type | solution.py:14
  20.3 0.0 all-gather.3.cloned.1.call-update
  20.3 0.0 reduce-scatter.2.cloned.1.call-start
  21.0 73.9 %all-gather.5.cloned.1.call-done = bf16[512,4096]{1,0:T(8,128)(2,1)} async-done(((bf16[128,4096]{1,0:T(8,128)(2,1)}), bf16[512,4096]{1,0:T(8,128)(2,1)}) %all-gather.5.cloned.1.call-update) | async-done | bytes 4194320 | tf_op jit(solution)/shard_map/all_gather | solution.py:34
  94.9 9.1 %convolution_convert_fusion.3 = bf16[512,1024]{1,0:T(8,128)(2,1)S(1)} fusion(bf16[512,4096]{1,0:T(8,128)(2,1)} %all-gather.5.cloned.1.call-done, bf16[4096,1024]{1,0:T(8,128)(2,1)} %param.14), kind=kOutput, calls=%fused_computation.22 | convolution fusion | flops 4295491584 | bytes 13631488 | tf_op jit(solution)/shard_map/dot_general | solution.py:35
  104.1 0.7 copy.13
  104.8 277.5 %all-gather.3.cloned.1.call-done = bf16[2048,4096]{1,0:T(8,128)(2,1)} async-done(((bf16[512,4096]{1,0:T(8,128)(2,1)}), bf16[2048,4096]{1,0:T(8,128)(2,1)}) %all-gather.3.cloned.1.call-update) | async-done | bytes 16777232 | tf_op jit(solution)/shard_map/all_gather | solution.py:37
  382.3 23.9 %convolution_convert_fusion.1 = bf16[2048,1024]{0,1:T(8,128)(2,1)} fusion(bf16[2048,4096]{1,0:T(8,128)(2,1)} %all-gather.3.cloned.1.call-done, bf16[4096,1024]{1,0:T(8,128)(2,1)} %param.15), kind=kOutput, calls=%fused_computation.14 | convolution fusion | flops 17181966336 | bytes 29360128 | tf_op jit(solution)/shard_map/dot_general | solution.py:38
  406.2 27.6 %fusion.17 = (f32[16,512]{1,0:T(8,128)S(1)}, f32[16,512,2048]{2,1,0:T(8,128)}) fusion(pred[2048]{0:T(1024)(128)(4,1)S(1)} %iota_compare_fusion, bf16[512,16,64]{0,2,1:T(8,128)(2,1)S(1)} %bitcast.23, bf16[2048,16,64]{0,2,1:T(8,128)(2,1)} %bitcast.24), kind=kOutput, calls=%fused_computation.30 | convolution fusion | flops 2197817344 | bytes 72386560 | tf_op jit(solution)/shard_map/sub | solution.py:47
  433.8 23.9 %convolution_convert_fusion.2 = bf16[2048,1024]{0,1:T(8,128)(2,1)} fusion(bf16[2048,4096]{1,0:T(8,128)(2,1)} %all-gather.3.cloned.1.call-done, bf16[4096,1024]{1,0:T(8,128)(2,1)} %param.16), kind=kOutput, calls=%fused_computation.15 | convolution fusion | flops 17181966336 | bytes 29360128 | tf_op jit(solution)/shard_map/dot_general | solution.py:39
  457.7 24.7 %fusion.13 = bf16[16,64,512]{2,1,0:T(8,128)(2,1)S(1)} fusion(bf16[2048,16,64]{0,2,1:T(8,128)(2,1)} %bitcast.25, f32[16,512,2048]{2,1,0:T(8,128)} %get-tuple-element.3, f32[16,512]{1,0:T(8,128)S(1)} %get-tuple-element.2), kind=kOutput, calls=%fused_computation.23 | convolution fusion | flops 2181562368 | bytes 72384512 | tf_op jit(solution)/shard_map/hqk,khd->qhd/dot_general | solution.py:49
  482.4 9.5 %convolution_convert_fusion = bf16[512,4096]{1,0:T(8,128)(2,1)} fusion(bf16[512,1024]{0,1:T(8,128)(2,1)S(1)} %bitcast.26, bf16[1024,4096]{1,0:T(8,128)(2,1)} %param.17), kind=kOutput, calls=%fused_computation.13 | convolution fusion | flops 4297064448 | bytes 13631488 | tf_op jit(solution)/shard_map/dot_general | solution.py:52
  491.9 0.0 reduce-scatter.2.cloned.1.call-update
  492.6 74.5 %reduce-scatter.2.cloned.1.call-done = bf16[128,4096]{1,0:T(8,128)(2,1)} async-done(((bf16[512,4096]{1,0:T(8,128)(2,1)}), bf16[128,4096]{1,0:T(8,128)(2,1)}) %reduce-scatter.2.cloned.1.call-update) | async-done | bytes 1048592 | tf_op jit(solution)/shard_map/reduce_scatter | solution.py:51
  567.0 2.5 select_convert_fusion
  (4 shorter events, 0.0 us)
Async XLA Ops:
  7.2 7.3 %copy-start = (f32[4096]{0:T(1024)S(1)}, f32[4096]{0:T(1024)}, u32[]{:S(2)}) copy-start(f32[4096]{0:T(1024)} %param.11) | copy-start | bytes 49156
  7.2 87.7 %all-gather.5.cloned.1.call-start = ((), (), s32[]{:S(2)}) async-start(), calls=%async_computation.2 | async-start | bytes 5242880 | tf_op jit(solution)/shard_map/all_gather | solution.py:34
  11.3 371.0 %all-gather.3.cloned.1.call-start = ((), (), s32[]{:S(2)}) async-start(), calls=%async_computation.1 | async-start | bytes 20971520 | tf_op jit(solution)/shard_map/all_gather | solution.py:37
  20.3 546.7 %reduce-scatter.2.cloned.1.call-start = ((), (), s32[]{:S(2)}) async-start(), calls=%async_computation.3 | async-start | bytes 5242880 | tf_op jit(solution)/shard_map/reduce_scatter | solution.py:51
Sparse Core Ops, SparseCore 0:
  11.4 83.4 all-gather.4
  97.1 285.2 all-gather.2
  492.0 74.9 reduce-scatter.1
where the time goes:
time: 576 us
  waiting for transfers between devices  426 us (74%)
  matrix products  119 us (21%)
  other arithmetic  15.5 us (3%)
  between operations  15.1 us (3%)
    all_gather x1, waiting for transfers between devices, shards(): segment = lax.all_gather(memory, 'tensor', axis=0, tiled=True)  278 us
    reduce_scatter x1, waiting for transfers between devices, shards(): lax.psum_scatter(jnp.dot(context, w_out, preferred_element_type=jnp.float...  74.5 us
    all_gather x1, waiting for transfers between devices, shards(): all_normed = lax.all_gather(normed, 'tensor', axis=0, tiled=True)  73.9 us
    sub x1, matrix products, shards(): weights = jax.nn.softmax(scores, axis=-1).astype(jnp.bfloat16)  27.6 us
    dot_general x1, matrix products, shards(): jnp.einsum('hqk,khd->qhd', weights, v_heads, preferred_element_type=jnp.f...  24.7 us
    dot_general x1, matrix products, shards(): jnp.dot(segment, w_key, preferred_element_type=jnp.float32)  23.9 us
    dot_general x1, matrix products, shards(): jnp.dot(segment, w_value, preferred_element_type=jnp.float32)  23.9 us
  transfers between devices with their start and end apart: 3, of which 3 were waited for; matrix products, arithmetic and copies ran while one was open for 3% of the time, Pallas kernels for 0%

commit v1 on v0

--- a/solution.py
+++ b/solution.py
@@ -6,6 +6,12 @@
 HEAD_DIM = 64
 ENC_LEN = 2048
 DEC_LEN = 512
+
+
+def joined_along(blocks, dim):
+    dims = list(blocks.shape[1:])
+    dims[dim] *= blocks.shape[0]
+    return jnp.moveaxis(blocks, 0, dim).reshape(dims)
 
 
 def rms_norm(values, gain):
@@ -31,7 +37,19 @@
     local_width = w_query.shape[1]
     local_heads = local_width // HEAD_DIM
     dec_rows = dec_hidden.shape[0]
-    all_normed = lax.all_gather(normed, "tensor", axis=0, tiled=True)
+    devices = lax.axis_size("tensor")
+    pairs = [(i, (i + 1) % devices) for i in range(devices)]
+    back = [(b, a) for a, b in pairs]
+    lower, upper = ([], [])
+    for step in range(devices - 1):
+        if step % 2 == 0:
+            lower.append(lax.ppermute(lower[-1] if lower else normed, "tensor", pairs))
+        else:
+            upper.append(lax.ppermute(upper[-1] if upper else normed, "tensor", back))
+    blocks = jnp.stack([*lower[::-1], normed, *upper])
+    shift = lax.axis_index("tensor") - len(lower)
+    blocks = blocks[(jnp.arange(devices) - shift) % devices]
+    all_normed = joined_along(blocks, 0)
     queries = jnp.dot(all_normed, w_query, preferred_element_type=jnp.float32).astype(jnp.bfloat16)
     q_heads = queries.reshape(DEC_LEN, local_heads, HEAD_DIM)
     segment = lax.all_gather(memory, "tensor", axis=0, tiled=True)

time: 576 us -> 556 us (0.965)
  waiting for transfers between devices: 426 us -> 352 us
  starting transfers between devices: 0.12 us -> 47.8 us
  local copies, waits for them, and re-layouts: 0.73 us -> 6.9 us
    all_gather x1, waiting for transfers between devices: 278 us -> 196 us  [shards(): segment = lax.all_gather(memory, 'tensor', axis=0, tiled=True)]
    ppermute x0 -> x3, waiting for transfers between devices: none -> 81.3 us  [the longest x2 60.3 us: shards(): lower.append(lax.ppermute(lower[-1] if lower else normed, 'tensor', pairs))]
    all_gather x1 -> x0, waiting for transfers between devices: 73.9 us -> none  [shards(): all_normed = lax.all_gather(normed, 'tensor', axis=0, tiled=True)]
    ppermute x0 -> x3, starting transfers between devices: none -> 47.7 us  [the longest x2 45.6 us: shards(): lower.append(lax.ppermute(lower[-1] if lower else normed, 'tensor', pairs))]
  transfers between devices with their start and end apart: 3 -> 5, of which waited for: 3 -> 5; matrix products, arithmetic and copies ran while one was open for 3% -> 3% of each run, Pallas kernels for 0% -> 0%
where the time goes in v1:
time: 556 us
  waiting for transfers between devices  352 us (63%)
  matrix products  119 us (21%)
  starting transfers between devices  47.8 us (9%)
  between operations  15.4 us (3%)
  other arithmetic  14.3 us (3%)
  local copies, waits for them, and re-layouts  6.9 us (1%)
    all_gather x1, waiting for transfers between devices, shards(): segment = lax.all_gather(memory, 'tensor', axis=0, tiled=True)  196 us
    reduce_scatter x1, waiting for transfers between devices, shards(): lax.psum_scatter(jnp.dot(context, w_out, preferred_element_type=jnp.float...  75.5 us
    ppermute x2, waiting for transfers between devices, shards(): lower.append(lax.ppermute(lower[-1] if lower else normed, 'tensor', pairs))  60.3 us
    ppermute x2, starting transfers between devices, shards(): lower.append(lax.ppermute(lower[-1] if lower else normed, 'tensor', pairs))  45.6 us
    sub x1, matrix products, shards(): weights = jax.nn.softmax(scores, axis=-1).astype(jnp.bfloat16)  27.5 us
    dot_general x1, matrix products, shards(): jnp.einsum('hqk,khd->qhd', weights, v_heads, preferred_element_type=jnp.f...  24.7 us
    dot_general x1, matrix products, shards(): jnp.dot(segment, w_key, preferred_element_type=jnp.float32)  23.9 us
    dot_general x1, matrix products, shards(): jnp.dot(segment, w_value, preferred_element_type=jnp.float32)  23.9 us
  transfers between devices with their start and end apart: 5, of which 5 were waited for; matrix products, arithmetic and copies ran while one was open for 3% of the time, Pallas kernels for 0%

profile of v1, /device:TPU:0, one launch (start us, length us, event | category | flops | bytes accessed | tf_op | source)
XLA Modules:
  0.0 555.7 jit_solution(11714157248687442645)
XLA Ops:
  7.2 3.2 fusion.7
  10.7 4.4 fusion.9
  15.1 1.1 copy-done.1
  16.2 0.3 fusion.10
  16.5 0.3 fusion.12
  16.9 3.1 collective-permute-start
  20.0 2.1 collective-permute-start.2
  22.8 35.1 %collective-permute-done = bf16[128,4096]{1,0:T(8,128)(2,1)S(1)} collective-permute-done((bf16[128,4096]{1,0:T(8,128)(2,1)S(1)}, bf16[128,4096]{1,0:T(8,128)(2,1)S(1)}, u32[]{:S(2)}, u32[]{:S(2)}) %collective-permute-start) | collective-permute-done | bytes 1048608 | tf_op jit(solution)/shard_map/ppermute | solution.py:46
  57.8 42.5 %collective-permute-start.1 = (bf16[128,4096]{1,0:T(8,128)(2,1)S(1)}, bf16[128,4096]{1,0:T(8,128)(2,1)S(1)}, u32[]{:S(2)}, u32[]{:S(2)}) collective-permute-start(bf16[128,4096]{1,0:T(8,128)(2,1)S(1)} %collective-permute-done), channel_id=1, source_target_pairs={{0,1},{1,2},{2,3},{3,0},{4,5},{5,6},{6,7},{7,4},{8,9},{9,10},{10,1... | collective-permute-start | bytes 3145736 | tf_op jit(solution)/shard_map/ppermute | solution.py:46
  100.4 0.3 fusion.33
  100.7 21.0 %collective-permute-done.2 = bf16[128,4096]{1,0:T(8,128)(2,1)} collective-permute-done((bf16[128,4096]{1,0:T(8,128)(2,1)S(1)}, bf16[128,4096]{1,0:T(8,128)(2,1)}, u32[]{:S(2)}, u32[]{:S(2)}) %collective-permute-start.2) | collective-permute-done | bytes 1048608 | tf_op jit(solution)/shard_map/ppermute | solution.py:48
  121.7 25.2 %collective-permute-done.1 = bf16[128,4096]{1,0:T(8,128)(2,1)S(1)} collective-permute-done((bf16[128,4096]{1,0:T(8,128)(2,1)S(1)}, bf16[128,4096]{1,0:T(8,128)(2,1)S(1)}, u32[]{:S(2)}, u32[]{:S(2)}) %collective-permute-start.1) | collective-permute-done | bytes 1048608 | tf_op jit(solution)/shard_map/ppermute | solution.py:46
  146.9 3.3 pad_maximum_fusion
  150.2 5.0 gather_fusion
  155.2 9.2 %convolution_convert_fusion.3 = bf16[512,1024]{1,0:T(8,128)(2,1)S(1)} fusion(bf16[512,4096]{1,0:T(8,128)(2,1)} %bitcast.31, bf16[4096,1024]{1,0:T(8,128)(2,1)} %param.14), kind=kOutput, calls=%fused_computation.24 | convolution fusion | flops 4295491584 | bytes 13631488 | tf_op jit(solution)/shard_map/dot_general | solution.py:53
  164.4 0.5 copy.13
  164.9 195.5 %all-gather.2.cloned.1.call-done = bf16[2048,4096]{1,0:T(8,128)(2,1)} async-done(((bf16[512,4096]{1,0:T(8,128)(2,1)}), bf16[2048,4096]{1,0:T(8,128)(2,1)}) %all-gather.2.cloned.1.call-update) | async-done | bytes 16777232 | tf_op jit(solution)/shard_map/all_gather | solution.py:55
  360.4 23.9 %convolution_convert_fusion.1 = bf16[2048,1024]{0,1:T(8,128)(2,1)} fusion(bf16[2048,4096]{1,0:T(8,128)(2,1)} %all-gather.2.cloned.1.call-done, bf16[4096,1024]{1,0:T(8,128)(2,1)} %param.15), kind=kOutput, calls=%fused_computation.16 | convolution fusion | flops 17181966336 | bytes 29360128 | tf_op jit(solution)/shard_map/dot_general | solution.py:56
  384.3 27.5 %fusion.19 = (f32[16,512]{1,0:T(8,128)S(1)}, f32[16,512,2048]{2,1,0:T(8,128)}) fusion(pred[2048]{0:T(1024)(128)(4,1)S(1)} %iota_compare_fusion, bf16[512,16,64]{0,2,1:T(8,128)(2,1)S(1)} %bitcast.32, bf16[2048,16,64]{0,2,1:T(8,128)(2,1)} %bitcast.35), kind=kOutput, calls=%fused_computation.39 | convolution fusion | flops 2197817344 | bytes 72386560 | tf_op jit(solution)/shard_map/sub | solution.py:65
  411.9 23.9 %convolution_convert_fusion.2 = bf16[2048,1024]{0,1:T(8,128)(2,1)} fusion(bf16[2048,4096]{1,0:T(8,128)(2,1)} %all-gather.2.cloned.1.call-done, bf16[4096,1024]{1,0:T(8,128)(2,1)} %param.16), kind=kOutput, calls=%fused_computation.17 | convolution fusion | flops 17181966336 | bytes 29360128 | tf_op jit(solution)/shard_map/dot_general | solution.py:57
  435.7 24.7 %fusion.13 = bf16[16,64,512]{2,1,0:T(8,128)(2,1)S(1)} fusion(bf16[2048,16,64]{0,2,1:T(8,128)(2,1)} %bitcast.36, f32[16,512,2048]{2,1,0:T(8,128)} %get-tuple-element.3, f32[16,512]{1,0:T(8,128)S(1)} %get-tuple-element.2), kind=kOutput, calls=%fused_computation.25 | convolution fusion | flops 2181562368 | bytes 72384512 | tf_op jit(solution)/shard_map/hqk,khd->qhd/dot_general | solution.py:67
  460.5 9.7 %convolution_convert_fusion = bf16[512,4096]{1,0:T(8,128)(2,1)} fusion(bf16[512,1024]{0,1:T(8,128)(2,1)S(1)} %bitcast.37, bf16[1024,4096]{1,0:T(8,128)(2,1)} %param.17), kind=kOutput, calls=%fused_computation.14 | convolution fusion | flops 4297064448 | bytes 13631488 | tf_op jit(solution)/shard_map/dot_general | solution.py:70
  470.9 75.5 %reduce-scatter.2.cloned.1.call-done = bf16[128,4096]{1,0:T(8,128)(2,1)} async-done(((bf16[512,4096]{1,0:T(8,128)(2,1)}), bf16[128,4096]{1,0:T(8,128)(2,1)}) %reduce-scatter.2.cloned.1.call-update) | async-done | bytes 1048592 | tf_op jit(solution)/shard_map/reduce_scatter | solution.py:69
  546.4 2.5 select_convert_fusion
  (15 shorter events, 0.4 us)
Async XLA Ops:
  7.2 353.3 %all-gather.2.cloned.1.call-start = ((), (), s32[]{:S(2)}) async-start(), calls=%async_computation.1 | async-start | bytes 20971520 | tf_op jit(solution)/shard_map/all_gather | solution.py:55
  7.2 3.5 copy-start
  15.0 1.2 copy-start.1
  15.0 1.5 copy-start.2
  15.0 531.4 %reduce-scatter.2.cloned.1.call-start = ((), (), s32[]{:S(2)}) async-start(), calls=%async_computation.2 | async-start | bytes 5242880 | tf_op jit(solution)/shard_map/reduce_scatter | solution.py:69
  16.9 41.0 %collective-permute-start = (bf16[128,4096]{1,0:T(8,128)(2,1)S(1)}, bf16[128,4096]{1,0:T(8,128)(2,1)S(1)}, u32[]{:S(2)}, u32[]{:S(2)}) collective-permute-start(bf16[128,4096]{1,0:T(8,128)(2,1)S(1)} %fusion.12), channel_id=1, source_target_pairs={{0,1},{1,2},{2,3},{3,0},{4,5},{5,6},{6,7},{7,4},{8,9},{9,10},{10,1... | collective-permute-start | bytes 3145736 | tf_op jit(solution)/shard_map/ppermute | solution.py:46
  20.0 101.7 %collective-permute-start.2 = (bf16[128,4096]{1,0:T(8,128)(2,1)S(1)}, bf16[128,4096]{1,0:T(8,128)(2,1)}, u32[]{:S(2)}, u32[]{:S(2)}) collective-permute-start(bf16[128,4096]{1,0:T(8,128)(2,1)S(1)} %fusion.12), channel_id=1, source_target_pairs={{1,0},{2,1},{3,2},{0,3},{5,4},{6,5},{7,6},{4,7},{9,8},{10,9},{11,1... | collective-permute-start | bytes 3145736 | tf_op jit(solution)/shard_map/ppermute | solution.py:48
  57.8 89.0 %collective-permute-start.1 = (bf16[128,4096]{1,0:T(8,128)(2,1)S(1)}, bf16[128,4096]{1,0:T(8,128)(2,1)S(1)}, u32[]{:S(2)}, u32[]{:S(2)}) collective-permute-start(bf16[128,4096]{1,0:T(8,128)(2,1)S(1)} %collective-permute-done), channel_id=1, source_target_pairs={{0,1},{1,2},{2,3},{3,0},{4,5},{5,6},{6,7},{7,4},{8,9},{9,10},{10,1... | collective-permute-start | bytes 3145736 | tf_op jit(solution)/shard_map/ppermute | solution.py:46
Sparse Core Ops, SparseCore 0:
  15.2 345.2 all-gather.1
  470.3 76.0 reduce-scatter.1
